TPU v7x, 32 devices: a whole 2x2x4 slice. The times are simulated.
32 devices in a mesh: px: 4 (over z), py: 8 (over y, x, core).
Axes of the slice: x: 2, y: 2, z: 4, core: 2. Of those that a mesh axis runs over, the one named last changes fastest.
Arguments:
- stiffness: float32 [9, 3, 3, 64, 1024], P(None, None, None, 'px', 'py'), may hold values from -3 to 9, as said below
- basis: float32 [32, 3, 64, 1024], P(None, None, 'px', 'py'), may hold values from -6 to 6
- current: float32 [3, 64, 1024], P(None, 'px', 'py'), may hold values from -12 to 12, as said below
Outputs:
- new_vectors: float32 [3, 3, 64, 1024], P(None, None, 'px', 'py')
- coefficients: float32 [3, 36], replicated
Inputs may be any that keep to these rules, and one draw needn't show every extreme that they name: `stiffness`: diagonal blocks of the centre coupling dominate each row. `current`: entries of order one.
All inputs are finite; a program needn't handle non-finite values.
Results may differ from a plain program's by a relative error of at most 0.0003.
Values sent between devices are 32-bit elements; how exact they have to be, the bound alone decides.
A program may use at most 64 MiB of HBM per device.

v0:
```python
import jax
import jax.numpy as jnp
from jax import lax
from jax.sharding import PartitionSpec as P

STEPS = 3
EPSILON = 1e-06


def with_halo(shard, sides, width):
    for axis, dim in sides:
        devices, length = (lax.axis_size(axis), shard.shape[dim])
        up = [(i, (i + 1) % devices) for i in range(devices - 1)]
        down = [(j, i) for i, j in up]
        last = lax.slice_in_dim(shard, length - width, length, axis=dim)
        initial = lax.slice_in_dim(shard, 0, width, axis=dim)
        before = lax.ppermute(last, axis, up)
        after = lax.ppermute(initial, axis, down)
        shard = jnp.concatenate([before, shard, after], axis=dim)
    return shard


def stencil(padded, stiffness):
    height = padded.shape[1] - 2
    breadth = padded.shape[2] - 2
    total = jnp.zeros((3, height, breadth), jnp.float32)
    for shift_x in range(3):
        for shift_y in range(3):
            shifted = padded[:, shift_x : shift_x + height, shift_y : shift_y + breadth]
            total = total + jnp.sum(stiffness[shift_x * 3 + shift_y] * shifted[None], axis=1)
    return total


def per_device(stiffness, basis, current):
    degrees = 3.0 * current.shape[1] * current.shape[2] * lax.axis_size("px") * lax.axis_size("py")
    count = basis.shape[0]
    records = []
    betas = []
    settled = []
    pending = current
    for step in range(STEPS):
        padded = with_halo(pending, (("px", 1), ("py", 2)), 1)
        image = stencil(padded, stiffness)
        local_new = [jnp.sum(member * image) for member in settled] + [jnp.sum(pending * image)]
        local_dots = jnp.concatenate(
            [
                jnp.einsum("mabc,abc->m", basis, image, precision=lax.Precision.HIGHEST),
                jnp.stack(local_new),
            ]
        )
        dots, square = lax.psum((local_dots, jnp.sum(pending * pending)), ("px", "py"))
        dots = dots / degrees
        if step == 0:
            scale = jnp.ones((), jnp.float32)
        else:
            scale = jnp.sqrt(square / degrees + EPSILON)
            betas.append(scale)
        vector = pending / scale
        settled.append(vector)
        weights = jnp.concatenate([dots[:-1] / scale, dots[-1:] / (scale * scale)])
        records.append(weights)
        subtract_image = image / scale
        result = subtract_image - jnp.einsum(
            "m,mabc->abc", weights[:count], basis, precision=lax.Precision.HIGHEST
        )
        for place in range(len(settled)):
            result = result - weights[count + place] * settled[place]
        pending = result
    square = lax.psum(jnp.sum(pending * pending), ("px", "py"))
    scale = jnp.sqrt(square / degrees + EPSILON)
    betas.append(scale)
    settled.append(pending / scale)
    produced = settled[1:]
    rows = []
    for step in range(STEPS):
        rows.append(
            jnp.concatenate(
                [records[step], betas[step][None], jnp.zeros((STEPS - 1 - step,), jnp.float32)]
            )
        )
    return (jnp.stack(produced), jnp.stack(rows))


def solution(mesh):
    in_specs = (P(None, None, None, "px", "py"), P(None, None, "px", "py"), P(None, "px", "py"))
    out_specs = (P(None, None, "px", "py"), P())
    return jax.shard_map(
        per_device, mesh=mesh, in_specs=in_specs, out_specs=out_specs, check_vma=False
    )
```

profile of v0, /device:TPU:0, one launch (start us, length us, event | category | flops | bytes accessed | tf_op | source)
XLA Modules:
  0.0 237.2 jit_solution(16599239941670386635)
XLA Ops:
  0.7 0.8 fusion.55
  1.5 1.3 collective-permute-start.1
  2.8 5.6 %collective-permute-start = (f32[3,1,128]{2,1,0:T(1,128)S(1)}, f32[3,1,128]{2,1,0:T(1,128)S(1)}, u32[]{:S(2)}, u32[]{:S(2)}) collective-permute-start(f32[3,1,128]{2,1,0:T(1,128)S(1)} %get-tuple-element.89), channel_id=1, source_target_pairs={{0,8},{8,16},{16,24},{1,9},{9,17},{17,25},{2,10},{10,18},{18,26},{... | collective-permute-start | bytes 4616 | tf_op jit(solution)/shard_map/ppermute | solution.py:17
  8.4 1.3 collective-permute-done
  9.7 0.7 pad_maximum_fusion.4
  10.5 1.3 collective-permute-start.3
  11.8 3.0 %collective-permute-start.2 = (f32[3,18,1]{2,1,0:T(8,128)S(1)}, f32[3,18,1]{2,1,0:T(8,128)S(1)}, u32[]{:S(2)}, u32[]{:S(2)}) collective-permute-start(f32[3,18,1]{2,1,0:T(8,128)S(1)} %get-tuple-element.69), channel_id=1, source_target_pairs={{0,1},{1,2},{2,3},{3,4},{4,5},{5,6},{6,7},{8,9},{9,10},{10,11},{11... | collective-permute-start | bytes 656 | tf_op jit(solution)/shard_map/ppermute | solution.py:17
  14.8 0.8 pad_maximum_fusion.11
  15.7 0.9 pad_maximum_fusion
  18.0 0.8 convolution_bitcast_fusion.2
  18.9 0.7 pad_maximum_fusion.14
  19.6 43.6 %psum.42 = f32[33]{0:T(128)S(1)} all-reduce(f32[33]{0:T(128)S(1)} %pad_maximum_fusion.14), channel_id=1, replica_groups=mesh['px'=4,'py'=8] {'px','py'}, use_global_device_ids=true, to_apply=%region_10.0 | all-reduce | flops 33 | bytes 264 | tf_op jit(solution)/shard_map/psum | solution.py:51
  65.1 1.3 collective-permute-start.5
  66.4 4.5 %collective-permute-start.4 = (f32[3,1,128]{2,1,0:T(1,128)S(1)}, f32[3,1,128]{2,1,0:T(1,128)S(1)}, u32[]{:S(2)}, u32[]{:S(2)}) collective-permute-start(f32[3,1,128]{2,1,0:T(1,128)S(1)} %get-tuple-element.85), channel_id=1, source_target_pairs={{0,8},{8,16},{16,24},{1,9},{9,17},{17,25},{2,10},{10,18},{18,26},{... | collective-permute-start | bytes 4616 | tf_op jit(solution)/shard_map/ppermute | solution.py:17
  71.0 1.3 collective-permute-done.4
  72.4 1.3 collective-permute-start.7
  73.7 3.0 %collective-permute-start.6 = (f32[3,18,1]{2,1,0:T(8,128)S(1)}, f32[3,18,1]{2,1,0:T(8,128)S(1)}, u32[]{:S(2)}, u32[]{:S(2)}) collective-permute-start(f32[3,18,1]{2,1,0:T(8,128)S(1)} %get-tuple-element.67), channel_id=1, source_target_pairs={{0,1},{1,2},{2,3},{3,4},{4,5},{5,6},{6,7},{8,9},{9,10},{10,11},{11... | collective-permute-start | bytes 656 | tf_op jit(solution)/shard_map/ppermute | solution.py:17
  76.7 0.8 collective-permute-done.6
  78.5 0.8 convolution_bitcast_fusion.1
  79.4 1.4 pad_maximum_fusion.15
  80.8 44.0 %all-reduce.1 = (f32[34]{0:T(128)S(1)}, f32[]{:T(128)}) all-reduce(f32[34]{0:T(128)S(1)} %pad_maximum_fusion.15, f32[]{:T(128)} %get-tuple-element.33), channel_id=1, replica_groups=mesh['px'=4,'py'=8] {'px','py'}, use_global_device_ids=true, to_apply=%region_24.0 | all-reduce | flops 35 | bytes 280 | tf_op jit(solution)/shard_map/psum | solution.py:51
  128.6 1.3 collective-permute-start.9
  129.9 4.5 %collective-permute-start.8 = (f32[3,1,128]{2,1,0:T(1,128)S(1)}, f32[3,1,128]{2,1,0:T(1,128)S(1)}, u32[]{:S(2)}, u32[]{:S(2)}) collective-permute-start(f32[3,1,128]{2,1,0:T(1,128)S(1)} %get-tuple-element.81), channel_id=1, source_target_pairs={{0,8},{8,16},{16,24},{1,9},{9,17},{17,25},{2,10},{10,18},{18,26},{... | collective-permute-start | bytes 4616 | tf_op jit(solution)/shard_map/ppermute | solution.py:17
  134.6 1.2 collective-permute-done.8
  135.9 1.3 collective-permute-start.11
  137.2 3.0 %collective-permute-start.10 = (f32[3,18,1]{2,1,0:T(8,128)S(1)}, f32[3,18,1]{2,1,0:T(8,128)S(1)}, u32[]{:S(2)}, u32[]{:S(2)}) collective-permute-start(f32[3,18,1]{2,1,0:T(8,128)S(1)} %get-tuple-element.65), channel_id=1, source_target_pairs={{0,1},{1,2},{2,3},{3,4},{4,5},{5,6},{6,7},{8,9},{9,10},{10,11},{11... | collective-permute-start | bytes 656 | tf_op jit(solution)/shard_map/ppermute | solution.py:17
  140.2 0.8 collective-permute-done.10
  142.0 0.8 convolution_bitcast_fusion
  142.9 1.9 pad_maximum_fusion.16
  144.8 44.1 %all-reduce = (f32[35]{0:T(128)S(1)}, f32[]{:T(128)}) all-reduce(f32[35]{0:T(128)S(1)} %pad_maximum_fusion.16, f32[]{:T(128)} %get-tuple-element.29), channel_id=1, replica_groups=mesh['px'=4,'py'=8] {'px','py'}, use_global_device_ids=true, to_apply=%region_39.0 | all-reduce | flops 36 | bytes 288 | tf_op jit(solution)/shard_map/psum | solution.py:51
  192.1 1.9 multiply_reduce_fusion
  194.0 41.2 %psum.47 = f32[]{:T(128)} all-reduce(f32[]{:T(128)} %get-tuple-element.40), channel_id=1, replica_groups=mesh['px'=4,'py'=8] {'px','py'}, use_global_device_ids=true, to_apply=%region_41.0 | all-reduce | flops 1 | bytes 8 | tf_op jit(solution)/shard_map/psum | solution.py:69
  (57 shorter events, 11.4 us)
Async XLA Ops:
  0.6 17.4 %copy-start = (f32[32,3,16,128]{3,2,1,0:T(8,128)S(1)}, f32[32,3,16,128]{3,2,1,0:T(8,128)}, u32[]{:S(2)}) copy-start(f32[32,3,16,128]{3,2,1,0:T(8,128)} %param.4) | copy-start | bytes 2359300
  0.6 16.1 %copy-start.1 = (f32[9,3,3,16,128]{4,3,2,1,0:T(8,128)S(1)}, f32[9,3,3,16,128]{4,3,2,1,0:T(8,128)}, u32[]{:S(2)}) copy-start(f32[9,3,3,16,128]{4,3,2,1,0:T(8,128)} %param.3) | copy-start | bytes 1990660
  1.5 6.9 %collective-permute-start.1 = (f32[3,1,128]{2,1,0:T(1,128)S(1)}, f32[3,1,128]{2,1,0:T(1,128)S(1)}, u32[]{:S(2)}, u32[]{:S(2)}) collective-permute-start(f32[3,1,128]{2,1,0:T(1,128)S(1)} %get-tuple-element.88), channel_id=1, source_target_pairs={{8,0},{16,8},{24,16},{9,1},{17,9},{25,17},{10,2},{18,10},{26,18},{... | collective-permute-start | bytes 4616 | tf_op jit(solution)/shard_map/ppermute | solution.py:18
  2.8 6.9 %collective-permute-start = (f32[3,1,128]{2,1,0:T(1,128)S(1)}, f32[3,1,128]{2,1,0:T(1,128)S(1)}, u32[]{:S(2)}, u32[]{:S(2)}) collective-permute-start(f32[3,1,128]{2,1,0:T(1,128)S(1)} %get-tuple-element.89), channel_id=1, source_target_pairs={{0,8},{8,16},{16,24},{1,9},{9,17},{17,25},{2,10},{10,18},{18,26},{... | collective-permute-start | bytes 4616 | tf_op jit(solution)/shard_map/ppermute | solution.py:17
  10.5 5.2 %collective-permute-start.3 = (f32[3,18,1]{2,1,0:T(8,128)S(1)}, f32[3,18,1]{2,1,0:T(8,128)S(1)}, u32[]{:S(2)}, u32[]{:S(2)}) collective-permute-start(f32[3,18,1]{2,1,0:T(8,128)S(1)} %get-tuple-element.68), channel_id=1, source_target_pairs={{1,0},{2,1},{3,2},{4,3},{5,4},{6,5},{7,6},{9,8},{10,9},{11,10},{12... | collective-permute-start | bytes 656 | tf_op jit(solution)/shard_map/ppermute | solution.py:18
  11.8 3.9 %collective-permute-start.2 = (f32[3,18,1]{2,1,0:T(8,128)S(1)}, f32[3,18,1]{2,1,0:T(8,128)S(1)}, u32[]{:S(2)}, u32[]{:S(2)}) collective-permute-start(f32[3,18,1]{2,1,0:T(8,128)S(1)} %get-tuple-element.69), channel_id=1, source_target_pairs={{0,1},{1,2},{2,3},{3,4},{4,5},{5,6},{6,7},{8,9},{9,10},{10,11},{11... | collective-permute-start | bytes 656 | tf_op jit(solution)/shard_map/ppermute | solution.py:17
  16.6 0.7 copy-start.2
  65.1 5.9 %collective-permute-start.5 = (f32[3,1,128]{2,1,0:T(1,128)S(1)}, f32[3,1,128]{2,1,0:T(1,128)S(1)}, u32[]{:S(2)}, u32[]{:S(2)}) collective-permute-start(f32[3,1,128]{2,1,0:T(1,128)S(1)} %get-tuple-element.84), channel_id=1, source_target_pairs={{8,0},{16,8},{24,16},{9,1},{17,9},{25,17},{10,2},{18,10},{26,18},{... | collective-permute-start | bytes 4616 | tf_op jit(solution)/shard_map/ppermute | solution.py:18
  66.4 5.8 %collective-permute-start.4 = (f32[3,1,128]{2,1,0:T(1,128)S(1)}, f32[3,1,128]{2,1,0:T(1,128)S(1)}, u32[]{:S(2)}, u32[]{:S(2)}) collective-permute-start(f32[3,1,128]{2,1,0:T(1,128)S(1)} %get-tuple-element.85), channel_id=1, source_target_pairs={{0,8},{8,16},{16,24},{1,9},{9,17},{17,25},{2,10},{10,18},{18,26},{... | collective-permute-start | bytes 4616 | tf_op jit(solution)/shard_map/ppermute | solution.py:17
  72.4 4.4 %collective-permute-start.7 = (f32[3,18,1]{2,1,0:T(8,128)S(1)}, f32[3,18,1]{2,1,0:T(8,128)S(1)}, u32[]{:S(2)}, u32[]{:S(2)}) collective-permute-start(f32[3,18,1]{2,1,0:T(8,128)S(1)} %get-tuple-element.66), channel_id=1, source_target_pairs={{1,0},{2,1},{3,2},{4,3},{5,4},{6,5},{7,6},{9,8},{10,9},{11,10},{12... | collective-permute-start | bytes 656 | tf_op jit(solution)/shard_map/ppermute | solution.py:18
  73.7 3.9 %collective-permute-start.6 = (f32[3,18,1]{2,1,0:T(8,128)S(1)}, f32[3,18,1]{2,1,0:T(8,128)S(1)}, u32[]{:S(2)}, u32[]{:S(2)}) collective-permute-start(f32[3,18,1]{2,1,0:T(8,128)S(1)} %get-tuple-element.67), channel_id=1, source_target_pairs={{0,1},{1,2},{2,3},{3,4},{4,5},{5,6},{6,7},{8,9},{9,10},{10,11},{11... | collective-permute-start | bytes 656 | tf_op jit(solution)/shard_map/ppermute | solution.py:17
  128.6 5.9 %collective-permute-start.9 = (f32[3,1,128]{2,1,0:T(1,128)S(1)}, f32[3,1,128]{2,1,0:T(1,128)S(1)}, u32[]{:S(2)}, u32[]{:S(2)}) collective-permute-start(f32[3,1,128]{2,1,0:T(1,128)S(1)} %get-tuple-element.80), channel_id=1, source_target_pairs={{8,0},{16,8},{24,16},{9,1},{17,9},{25,17},{10,2},{18,10},{26,18},{... | collective-permute-start | bytes 4616 | tf_op jit(solution)/shard_map/ppermute | solution.py:18
  129.9 5.8 %collective-permute-start.8 = (f32[3,1,128]{2,1,0:T(1,128)S(1)}, f32[3,1,128]{2,1,0:T(1,128)S(1)}, u32[]{:S(2)}, u32[]{:S(2)}) collective-permute-start(f32[3,1,128]{2,1,0:T(1,128)S(1)} %get-tuple-element.81), channel_id=1, source_target_pairs={{0,8},{8,16},{16,24},{1,9},{9,17},{17,25},{2,10},{10,18},{18,26},{... | collective-permute-start | bytes 4616 | tf_op jit(solution)/shard_map/ppermute | solution.py:17
  135.9 4.4 %collective-permute-start.11 = (f32[3,18,1]{2,1,0:T(8,128)S(1)}, f32[3,18,1]{2,1,0:T(8,128)S(1)}, u32[]{:S(2)}, u32[]{:S(2)}) collective-permute-start(f32[3,18,1]{2,1,0:T(8,128)S(1)} %get-tuple-element.64), channel_id=1, source_target_pairs={{1,0},{2,1},{3,2},{4,3},{5,4},{6,5},{7,6},{9,8},{10,9},{11,10},{12... | collective-permute-start | bytes 656 | tf_op jit(solution)/shard_map/ppermute | solution.py:18
  137.2 3.9 %collective-permute-start.10 = (f32[3,18,1]{2,1,0:T(8,128)S(1)}, f32[3,18,1]{2,1,0:T(8,128)S(1)}, u32[]{:S(2)}, u32[]{:S(2)}) collective-permute-start(f32[3,18,1]{2,1,0:T(8,128)S(1)} %get-tuple-element.65), channel_id=1, source_target_pairs={{0,1},{1,2},{2,3},{3,4},{4,5},{5,6},{6,7},{8,9},{9,10},{10,11},{11... | collective-permute-start | bytes 656 | tf_op jit(solution)/shard_map/ppermute | solution.py:17
where the time goes:
time: 238 us; the launch traced here: 237 us
  blocking collectives  173 us (73%)
  starting transfers between devices  31.5 us (13%)
  other arithmetic  13.6 us (6%)
  waiting for transfers between devices  5.4 us (2%)
  local copies, waits for them, and re-layouts  5.01 us (2%)
  matrix products  4.49 us (2%)
  between operations  4.26 us (2%)
    psum x3, blocking collectives, per_device(): lax.psum((local_dots, jnp.sum(pending * pending)), ('px', 'py'))  132 us
    psum x1, blocking collectives, per_device(): square = lax.psum(jnp.sum(pending * pending), ('px', 'py'))  41.2 us
    ppermute x6, starting transfers between devices, with_halo(): before = lax.ppermute(last, axis, up)  23.8 us
    ppermute x6, starting transfers between devices, with_halo(): after = lax.ppermute(initial, axis, down)  7.72 us
    ppermute x6, waiting for transfers between devices, with_halo(): before = lax.ppermute(last, axis, up)  5.38 us
  transfers between devices with their start and end apart: 12, of which 5 were waited for; matrix products, arithmetic and copies ran while one was open for 0% of the time, Pallas kernels for 0%

commit v1 on v0

--- a/solution.py
+++ b/solution.py
@@ -48,7 +48,7 @@
                 jnp.stack(local_new),
             ]
         )
-        dots, square = lax.psum((local_dots, jnp.sum(pending * pending)), ("px", "py"))
+        dots, square = lax.psum(lax.psum((local_dots, jnp.sum(pending * pending)), "py"), "px")
         dots = dots / degrees
         if step == 0:
             scale = jnp.ones((), jnp.float32)

time: 238 us -> 184 us (0.77)
  blocking collectives: 173 us -> 118 us
    psum x3 -> x6, blocking collectives: 132 us -> 78.6 us  [the longest x3 43.3 us: per_device(): lax.psum((local_dots, jnp.sum(pending * pending)), 'py')]
  transfers between devices with their start and end apart: 12 -> 12, of which waited for: 5 -> 5; matrix products, arithmetic and copies ran while one was open for 0% -> 1% of each run, Pallas kernels for 0% -> 0%
where the time goes in v1:
time: 184 us; the launch traced here: 183 us
  blocking collectives  118 us (64%)
  starting transfers between devices  31.5 us (17%)
  other arithmetic  13.6 us (7%)
  waiting for transfers between devices  5.4 us (3%)
  local copies, waits for them, and re-layouts  5.01 us (3%)
  matrix products  4.49 us (2%)
  between operations  4.39 us (2%)
    psum x3, blocking collectives, per_device(): lax.psum((local_dots, jnp.sum(pending * pending)), 'py')  43.3 us
    psum x1, blocking collectives, per_device(): square = lax.psum(jnp.sum(pending * pending), ('px', 'py'))  39.7 us
    psum x3, blocking collectives, per_device(): lax.psum(lax.psum((local_dots, jnp.sum(pending * pending)), 'py'), 'px')  35.2 us
    ppermute x6, starting transfers between devices, with_halo(): before = lax.ppermute(last, axis, up)  23.8 us
    ppermute x6, starting transfers between devices, with_halo(): after = lax.ppermute(initial, axis, down)  7.72 us
    ppermute x6, waiting for transfers between devices, with_halo(): before = lax.ppermute(last, axis, up)  5.38 us
    concatenate x3, other arithmetic, per_device(): jnp.concatenate([jnp.einsum('mabc,abc->m', basis, image, precision=lax.Pr...  4.08 us
  transfers between devices with their start and end apart: 12, of which 5 were waited for; matrix products, arithmetic and copies ran while one was open for 1% of the time, Pallas kernels for 0%

profile of v1, /device:TPU:0, one launch (start us, length us, event | category | flops | bytes accessed | tf_op | source)
XLA Modules:
  0.0 182.7 jit_solution(12064552134735901182)
XLA Ops:
  0.7 0.8 fusion.55
  1.5 1.3 collective-permute-start.1
  2.8 5.6 %collective-permute-start = (f32[3,1,128]{2,1,0:T(1,128)S(1)}, f32[3,1,128]{2,1,0:T(1,128)S(1)}, u32[]{:S(2)}, u32[]{:S(2)}) collective-permute-start(f32[3,1,128]{2,1,0:T(1,128)S(1)} %get-tuple-element.93), channel_id=1, source_target_pairs={{0,8},{8,16},{16,24},{1,9},{9,17},{17,25},{2,10},{10,18},{18,26},{... | collective-permute-start | bytes 4616 | tf_op jit(solution)/shard_map/ppermute | solution.py:17
  8.4 1.3 collective-permute-done
  10.5 1.3 collective-permute-start.3
  11.8 3.0 %collective-permute-start.2 = (f32[3,18,1]{2,1,0:T(8,128)S(1)}, f32[3,18,1]{2,1,0:T(8,128)S(1)}, u32[]{:S(2)}, u32[]{:S(2)}) collective-permute-start(f32[3,18,1]{2,1,0:T(8,128)S(1)} %get-tuple-element.73), channel_id=1, source_target_pairs={{0,1},{1,2},{2,3},{3,4},{4,5},{5,6},{6,7},{8,9},{9,10},{10,11},{11... | collective-permute-start | bytes 656 | tf_op jit(solution)/shard_map/ppermute | solution.py:17
  14.8 0.8 pad_maximum_fusion.11
  15.7 0.9 pad_maximum_fusion
  18.0 0.8 convolution_bitcast_fusion.2
  19.6 14.6 %psum.77 = f32[33]{0:T(128)S(1)} all-reduce(f32[33]{0:T(128)S(1)} %pad_maximum_fusion.14), channel_id=1, replica_groups=mesh['px'=4,'py'=8] {'py'}, use_global_device_ids=true, to_apply=%region_10.0 | all-reduce | flops 33 | bytes 264 | tf_op jit(solution)/shard_map/psum | solution.py:51
  34.2 12.6 %psum.78 = f32[33]{0:T(128)S(1)} all-reduce(f32[33]{0:T(128)S(1)} %psum.77), channel_id=1, replica_groups=mesh['px'=4,'py'=8] {'px'}, use_global_device_ids=true, to_apply=%region_11.0 | all-reduce | flops 33 | bytes 264 | tf_op jit(solution)/shard_map/psum | solution.py:51
  48.8 1.3 collective-permute-start.5
  50.1 4.5 %collective-permute-start.4 = (f32[3,1,128]{2,1,0:T(1,128)S(1)}, f32[3,1,128]{2,1,0:T(1,128)S(1)}, u32[]{:S(2)}, u32[]{:S(2)}) collective-permute-start(f32[3,1,128]{2,1,0:T(1,128)S(1)} %get-tuple-element.89), channel_id=1, source_target_pairs={{0,8},{8,16},{16,24},{1,9},{9,17},{17,25},{2,10},{10,18},{18,26},{... | collective-permute-start | bytes 4616 | tf_op jit(solution)/shard_map/ppermute | solution.py:17
  54.6 1.3 collective-permute-done.4
  56.0 1.3 collective-permute-start.7
  57.3 3.0 %collective-permute-start.6 = (f32[3,18,1]{2,1,0:T(8,128)S(1)}, f32[3,18,1]{2,1,0:T(8,128)S(1)}, u32[]{:S(2)}, u32[]{:S(2)}) collective-permute-start(f32[3,18,1]{2,1,0:T(8,128)S(1)} %get-tuple-element.71), channel_id=1, source_target_pairs={{0,1},{1,2},{2,3},{3,4},{4,5},{5,6},{6,7},{8,9},{9,10},{10,11},{11... | collective-permute-start | bytes 656 | tf_op jit(solution)/shard_map/ppermute | solution.py:17
  62.2 0.8 convolution_bitcast_fusion.1
  63.0 1.4 pad_maximum_fusion.15
  64.4 13.4 %all-reduce.1 = (f32[34]{0:T(128)S(1)}, f32[]{:T(128)}) all-reduce(f32[34]{0:T(128)S(1)} %pad_maximum_fusion.15, f32[]{:T(128)} %get-tuple-element.33), channel_id=1, replica_groups=mesh['px'=4,'py'=8] {'py'}, use_global_device_ids=true, to_apply=%region_26.0 | all-reduce | flops 35 | bytes 280 | tf_op jit(solution)/shard_map/psum | solution.py:51
  77.9 11.2 %all-reduce.3 = (f32[34]{0:T(128)S(1)}, f32[]{:T(128)}) all-reduce(f32[34]{0:T(128)S(1)} %get-tuple-element.38, f32[]{:T(128)} %get-tuple-element.39), channel_id=1, replica_groups=mesh['px'=4,'py'=8] {'px'}, use_global_device_ids=true, to_apply=%region_27.0 | all-reduce | flops 35 | bytes 280 | tf_op jit(solution)/shard_map/psum | solution.py:51
  92.9 1.3 collective-permute-start.9
  94.2 4.5 %collective-permute-start.8 = (f32[3,1,128]{2,1,0:T(1,128)S(1)}, f32[3,1,128]{2,1,0:T(1,128)S(1)}, u32[]{:S(2)}, u32[]{:S(2)}) collective-permute-start(f32[3,1,128]{2,1,0:T(1,128)S(1)} %get-tuple-element.85), channel_id=1, source_target_pairs={{0,8},{8,16},{16,24},{1,9},{9,17},{17,25},{2,10},{10,18},{18,26},{... | collective-permute-start | bytes 4616 | tf_op jit(solution)/shard_map/ppermute | solution.py:17
  98.9 1.2 collective-permute-done.8
  100.1 1.3 collective-permute-start.11
  101.4 3.0 %collective-permute-start.10 = (f32[3,18,1]{2,1,0:T(8,128)S(1)}, f32[3,18,1]{2,1,0:T(8,128)S(1)}, u32[]{:S(2)}, u32[]{:S(2)}) collective-permute-start(f32[3,18,1]{2,1,0:T(8,128)S(1)} %get-tuple-element.69), channel_id=1, source_target_pairs={{0,1},{1,2},{2,3},{3,4},{4,5},{5,6},{6,7},{8,9},{9,10},{10,11},{11... | collective-permute-start | bytes 656 | tf_op jit(solution)/shard_map/ppermute | solution.py:17
  104.5 0.8 collective-permute-done.10
  106.3 0.8 convolution_bitcast_fusion
  107.1 1.9 %pad_maximum_fusion.16 = f32[35]{0:T(128)S(1)} fusion(f32[1]{0:T(128)} %bitcast.40, f32[1]{0:T(128)} %bitcast.39, f32[1]{0:T(128)} %bitcast.38, f32[32]{0:T(128)S(1)} %convolution_bitcast_fusion), kind=kLoop, calls=%fused_computation.104 | loop fusion | flops 105 | bytes 280 | tf_op jit(solution)/shard_map/concatenate | solution.py:45
  109.0 15.3 %all-reduce = (f32[35]{0:T(128)S(1)}, f32[]{:T(128)}) all-reduce(f32[35]{0:T(128)S(1)} %pad_maximum_fusion.16, f32[]{:T(128)} %get-tuple-element.29), channel_id=1, replica_groups=mesh['px'=4,'py'=8] {'py'}, use_global_device_ids=true, to_apply=%region_43.0 | all-reduce | flops 36 | bytes 288 | tf_op jit(solution)/shard_map/psum | solution.py:51
  124.4 11.3 %all-reduce.2 = (f32[35]{0:T(128)S(1)}, f32[]{:T(128)}) all-reduce(f32[35]{0:T(128)S(1)} %get-tuple-element.36, f32[]{:T(128)} %get-tuple-element.37), channel_id=1, replica_groups=mesh['px'=4,'py'=8] {'px'}, use_global_device_ids=true, to_apply=%region_44.0 | all-reduce | flops 36 | bytes 288 | tf_op jit(solution)/shard_map/psum | solution.py:51
  139.0 1.9 %multiply_reduce_fusion = (f32[]{:T(128)}, f32[3,16,128]{2,1,0:T(8,128)S(1)}, f32[1,3,16,128]{3,2,1,0:T(8,128)S(1)}) fusion(f32[3,16,128]{2,1,0:T(8,128)S(1)} %multiply_subtract_fusion.1, f32[]{:T(128)} %bitcast.48, f32[3,16,128]{2,1,0:T(8,128)S(1)} %multiply_subtract_fusion.2, f32[]{:T(128)} %sqrt.9, f32[]{:T(128)} %bitcast.46, ...), kind=kLoop, calls=%fused_computation.83 | loop fusion | flops 73727 | bytes 172056 | tf_op jit(solution)/shard_map/reduce_sum | solution.py:69
  140.9 39.7 %psum.87 = f32[]{:T(128)} all-reduce(f32[]{:T(128)} %get-tuple-element.44), channel_id=1, replica_groups=mesh['px'=4,'py'=8] {'px','py'}, use_global_device_ids=true, to_apply=%region_46.0 | all-reduce | flops 1 | bytes 8 | tf_op jit(solution)/shard_map/psum | solution.py:69
  (60 shorter events, 13.7 us)
Async XLA Ops:
  0.6 17.4 %copy-start = (f32[32,3,16,128]{3,2,1,0:T(8,128)S(1)}, f32[32,3,16,128]{3,2,1,0:T(8,128)}, u32[]{:S(2)}) copy-start(f32[32,3,16,128]{3,2,1,0:T(8,128)} %param.4) | copy-start | bytes 2359300
  0.6 16.1 %copy-start.1 = (f32[9,3,3,16,128]{4,3,2,1,0:T(8,128)S(1)}, f32[9,3,3,16,128]{4,3,2,1,0:T(8,128)}, u32[]{:S(2)}) copy-start(f32[9,3,3,16,128]{4,3,2,1,0:T(8,128)} %param.3) | copy-start | bytes 1990660
  1.5 6.9 %collective-permute-start.1 = (f32[3,1,128]{2,1,0:T(1,128)S(1)}, f32[3,1,128]{2,1,0:T(1,128)S(1)}, u32[]{:S(2)}, u32[]{:S(2)}) collective-permute-start(f32[3,1,128]{2,1,0:T(1,128)S(1)} %get-tuple-element.92), channel_id=1, source_target_pairs={{8,0},{16,8},{24,16},{9,1},{17,9},{25,17},{10,2},{18,10},{26,18},{... | collective-permute-start | bytes 4616 | tf_op jit(solution)/shard_map/ppermute | solution.py:18
  2.8 6.9 %collective-permute-start = (f32[3,1,128]{2,1,0:T(1,128)S(1)}, f32[3,1,128]{2,1,0:T(1,128)S(1)}, u32[]{:S(2)}, u32[]{:S(2)}) collective-permute-start(f32[3,1,128]{2,1,0:T(1,128)S(1)} %get-tuple-element.93), channel_id=1, source_target_pairs={{0,8},{8,16},{16,24},{1,9},{9,17},{17,25},{2,10},{10,18},{18,26},{... | collective-permute-start | bytes 4616 | tf_op jit(solution)/shard_map/ppermute | solution.py:17
  10.5 5.2 %collective-permute-start.3 = (f32[3,18,1]{2,1,0:T(8,128)S(1)}, f32[3,18,1]{2,1,0:T(8,128)S(1)}, u32[]{:S(2)}, u32[]{:S(2)}) collective-permute-start(f32[3,18,1]{2,1,0:T(8,128)S(1)} %get-tuple-element.72), channel_id=1, source_target_pairs={{1,0},{2,1},{3,2},{4,3},{5,4},{6,5},{7,6},{9,8},{10,9},{11,10},{12... | collective-permute-start | bytes 656 | tf_op jit(solution)/shard_map/ppermute | solution.py:18
  11.8 3.9 %collective-permute-start.2 = (f32[3,18,1]{2,1,0:T(8,128)S(1)}, f32[3,18,1]{2,1,0:T(8,128)S(1)}, u32[]{:S(2)}, u32[]{:S(2)}) collective-permute-start(f32[3,18,1]{2,1,0:T(8,128)S(1)} %get-tuple-element.73), channel_id=1, source_target_pairs={{0,1},{1,2},{2,3},{3,4},{4,5},{5,6},{6,7},{8,9},{9,10},{10,11},{11... | collective-permute-start | bytes 656 | tf_op jit(solution)/shard_map/ppermute | solution.py:17
  16.6 0.7 copy-start.2
  48.8 5.9 %collective-permute-start.5 = (f32[3,1,128]{2,1,0:T(1,128)S(1)}, f32[3,1,128]{2,1,0:T(1,128)S(1)}, u32[]{:S(2)}, u32[]{:S(2)}) collective-permute-start(f32[3,1,128]{2,1,0:T(1,128)S(1)} %get-tuple-element.88), channel_id=1, source_target_pairs={{8,0},{16,8},{24,16},{9,1},{17,9},{25,17},{10,2},{18,10},{26,18},{... | collective-permute-start | bytes 4616 | tf_op jit(solution)/shard_map/ppermute | solution.py:18
  50.1 5.8 %collective-permute-start.4 = (f32[3,1,128]{2,1,0:T(1,128)S(1)}, f32[3,1,128]{2,1,0:T(1,128)S(1)}, u32[]{:S(2)}, u32[]{:S(2)}) collective-permute-start(f32[3,1,128]{2,1,0:T(1,128)S(1)} %get-tuple-element.89), channel_id=1, source_target_pairs={{0,8},{8,16},{16,24},{1,9},{9,17},{17,25},{2,10},{10,18},{18,26},{... | collective-permute-start | bytes 4616 | tf_op jit(solution)/shard_map/ppermute | solution.py:17
  56.0 4.4 %collective-permute-start.7 = (f32[3,18,1]{2,1,0:T(8,128)S(1)}, f32[3,18,1]{2,1,0:T(8,128)S(1)}, u32[]{:S(2)}, u32[]{:S(2)}) collective-permute-start(f32[3,18,1]{2,1,0:T(8,128)S(1)} %get-tuple-element.70), channel_id=1, source_target_pairs={{1,0},{2,1},{3,2},{4,3},{5,4},{6,5},{7,6},{9,8},{10,9},{11,10},{12... | collective-permute-start | bytes 656 | tf_op jit(solution)/shard_map/ppermute | solution.py:18
  57.3 3.9 %collective-permute-start.6 = (f32[3,18,1]{2,1,0:T(8,128)S(1)}, f32[3,18,1]{2,1,0:T(8,128)S(1)}, u32[]{:S(2)}, u32[]{:S(2)}) collective-permute-start(f32[3,18,1]{2,1,0:T(8,128)S(1)} %get-tuple-element.71), channel_id=1, source_target_pairs={{0,1},{1,2},{2,3},{3,4},{4,5},{5,6},{6,7},{8,9},{9,10},{10,11},{11... | collective-permute-start | bytes 656 | tf_op jit(solution)/shard_map/ppermute | solution.py:17
  92.9 5.9 %collective-permute-start.9 = (f32[3,1,128]{2,1,0:T(1,128)S(1)}, f32[3,1,128]{2,1,0:T(1,128)S(1)}, u32[]{:S(2)}, u32[]{:S(2)}) collective-permute-start(f32[3,1,128]{2,1,0:T(1,128)S(1)} %get-tuple-element.84), channel_id=1, source_target_pairs={{8,0},{16,8},{24,16},{9,1},{17,9},{25,17},{10,2},{18,10},{26,18},{... | collective-permute-start | bytes 4616 | tf_op jit(solution)/shard_map/ppermute | solution.py:18
  94.2 5.8 %collective-permute-start.8 = (f32[3,1,128]{2,1,0:T(1,128)S(1)}, f32[3,1,128]{2,1,0:T(1,128)S(1)}, u32[]{:S(2)}, u32[]{:S(2)}) collective-permute-start(f32[3,1,128]{2,1,0:T(1,128)S(1)} %get-tuple-element.85), channel_id=1, source_target_pairs={{0,8},{8,16},{16,24},{1,9},{9,17},{17,25},{2,10},{10,18},{18,26},{... | collective-permute-start | bytes 4616 | tf_op jit(solution)/shard_map/ppermute | solution.py:17
  100.1 4.4 %collective-permute-start.11 = (f32[3,18,1]{2,1,0:T(8,128)S(1)}, f32[3,18,1]{2,1,0:T(8,128)S(1)}, u32[]{:S(2)}, u32[]{:S(2)}) collective-permute-start(f32[3,18,1]{2,1,0:T(8,128)S(1)} %get-tuple-element.68), channel_id=1, source_target_pairs={{1,0},{2,1},{3,2},{4,3},{5,4},{6,5},{7,6},{9,8},{10,9},{11,10},{12... | collective-permute-start | bytes 656 | tf_op jit(solution)/shard_map/ppermute | solution.py:18
  101.4 3.9 %collective-permute-start.10 = (f32[3,18,1]{2,1,0:T(8,128)S(1)}, f32[3,18,1]{2,1,0:T(8,128)S(1)}, u32[]{:S(2)}, u32[]{:S(2)}) collective-permute-start(f32[3,18,1]{2,1,0:T(8,128)S(1)} %get-tuple-element.69), channel_id=1, source_target_pairs={{0,1},{1,2},{2,3},{3,4},{4,5},{5,6},{6,7},{8,9},{9,10},{10,11},{11... | collective-permute-start | bytes 656 | tf_op jit(solution)/shard_map/ppermute | solution.py:17
